TPU v7x, 32 devices: a whole 2x2x4 slice. The times are simulated.
32 devices in a mesh: ctx: 8 (over z, y), head: 4 (over x, core).
Axes of the slice: x: 2, y: 2, z: 4, core: 2. Of those that a mesh axis runs over, the one named last changes fastest.
Arguments:
- queries: bfloat16 [1024, 64, 128], P('ctx', 'head'), may hold values from -90 to 90
- key_states: bfloat16 [1024, 8, 128], P('ctx', 'head'), may hold values from -4.5 to 4.5
- value_states: bfloat16 [1024, 8, 128], P('ctx', 'head'), may hold values from -6 to 6
- chosen: int32 [2, 4], replicated, may hold values from 0 to 1, as said below
- valid_count: int32 [2], replicated, may hold values from 1 to 2, as said below
Outputs:
- attn_out: bfloat16 [1024, 64, 128], P('ctx', 'head')
- key_mass: float32 [64, 1024], P('head', 'ctx')
Inputs may be any that keep to these rules, and one draw needn't show every extreme that they name: `chosen`: row i lists block i first; if valid_count[i] >= 2, block 0 second; the next valid_count[i] - 2 entries are distinct blocks from 1 to i - 1; entries from position valid_count[i] on equal i. valid_count[i] is at most min(4, i + 1), and the last block's count is min(4, 2).
All inputs are finite; a program needn't handle non-finite values.
Results may differ from a plain program's by a relative error of at most 0.0046.
Values may be sent and summed in bfloat16 or wider, within the bound.
A program may use at most 64 MiB of HBM per device.

v0:
```python
import math

import jax
import jax.numpy as jnp
from jax import lax
from jax.sharding import PartitionSpec as P

BLOCK = 512


def from_partner(value, axis, bit):
    mask = 2**bit
    pairs = [(source, source ^ mask) for source in range(lax.axis_size(axis))]
    return lax.ppermute(value, axis, pairs)


def on_device(queries, key_states, value_states, chosen, valid_count):
    ctx_size = lax.axis_size("ctx")
    my_index = lax.axis_index("ctx")
    token_count = queries.shape[0]
    query_heads = queries.shape[1]
    head_depth = queries.shape[2]
    kv_total = key_states.shape[1]
    groups = query_heads // kv_total
    slot_total = chosen.shape[1]
    split_count = BLOCK // token_count
    quarter = token_count // split_count
    my_block = my_index // split_count
    my_member = my_index % split_count
    listed = chosen[my_block]
    slot_ids = jnp.arange(slot_total)
    slot_valid = slot_ids < valid_count[my_block]
    owners = jnp.arange(ctx_size) // split_count
    wanted = jnp.any(
        (slot_ids[None, :] < valid_count[owners][:, None]) & (chosen[owners] == my_block), axis=1
    )
    stacked = jnp.stack([key_states, value_states]).reshape(
        2, 1, split_count, quarter, kv_total, head_depth
    )
    outgoing = jnp.broadcast_to(
        stacked, (2, ctx_size // split_count, split_count, quarter, kv_total, head_depth)
    )
    outgoing = outgoing.reshape(2, ctx_size, quarter, kv_total, head_depth)
    outgoing = jnp.where(wanted[None, :, None, None, None], outgoing, jnp.zeros((), outgoing.dtype))
    incoming = lax.all_to_all(outgoing, "ctx", split_axis=1, concat_axis=1, tiled=True)
    sources = (listed[:, None] * split_count + jnp.arange(split_count)[None, :]).reshape(-1)
    fetched = jnp.take(incoming, sources, axis=1)
    bit_total = split_count.bit_length() - 1
    for bit_index in range(bit_total):
        partner = from_partner(fetched, "ctx", bit_index)
        is_lower = my_member // 2**bit_index % 2 == 0
        fetched = jnp.where(
            is_lower,
            jnp.concatenate([fetched, partner], axis=2),
            jnp.concatenate([partner, fetched], axis=2),
        )
    fetched = fetched.reshape(2, slot_total * BLOCK, kv_total, head_depth)
    by_head = jnp.transpose(fetched, (0, 2, 1, 3))
    query_pos = my_index * token_count + jnp.arange(token_count)
    score_scale = 1.0 / math.sqrt(head_depth)
    grouped = queries.reshape(token_count, kv_total, groups, head_depth)
    offsets = jnp.arange(BLOCK)
    key_pos = (listed[:, None] * BLOCK + offsets[None, :]).reshape(-1)
    key_block = jnp.repeat(listed, BLOCK)
    key_valid = jnp.repeat(slot_valid, BLOCK)
    visibility = key_valid[None, :] & (
        (key_block[None, :] < my_block) | (key_pos[None, :] <= query_pos[:, None])
    )
    contract_last = (((1,), (1,)), ((), ()))
    head_outputs = []
    head_masses = []
    for kv_head in range(kv_total):
        key_head = by_head[0, kv_head]
        value_head = by_head[1, kv_head]
        for group_index in range(groups):
            raw_scores = (
                lax.dot_general(
                    grouped[:, kv_head, group_index],
                    key_head,
                    contract_last,
                    preferred_element_type=jnp.float32,
                )
                * score_scale
            )
            scores = jnp.where(visibility, raw_scores, -jnp.inf)
            highest = jnp.max(scores, axis=-1, keepdims=True)
            raised = jnp.exp(scores - highest)
            attention = raised / jnp.sum(raised, axis=-1, keepdims=True)
            head_outputs.append(
                jnp.dot(
                    attention.astype(jnp.bfloat16), value_head, preferred_element_type=jnp.float32
                )
            )
            head_masses.append(jnp.sum(attention, axis=0).reshape(slot_total, BLOCK))
    attn_out = jnp.stack(head_outputs, axis=1).astype(jnp.bfloat16)
    contrib = jnp.stack(head_masses, axis=1).reshape(
        slot_total, query_heads, split_count, token_count
    )
    contrib = jnp.transpose(contrib, (0, 2, 1, 3)).reshape(
        slot_total * split_count, query_heads, token_count
    )
    landing = jnp.zeros((ctx_size, query_heads, token_count), jnp.float32).at[sources].add(contrib)
    key_mass = lax.psum_scatter(landing, "ctx", scatter_dimension=0, tiled=True).reshape(
        query_heads, token_count
    )
    return (attn_out, key_mass)


def solution(mesh):
    in_specs = (P("ctx", "head", None), P("ctx", "head", None), P("ctx", "head", None), P(), P())
    out_specs = (P("ctx", "head", None), P("head", "ctx"))
    return jax.shard_map(
        on_device, mesh=mesh, in_specs=in_specs, out_specs=out_specs, check_vma=False
    )
```

profile of v0, /device:TPU:0, one launch (start us, length us, event | category | flops | bytes accessed | tf_op | source)
XLA Modules:
  0.0 163.1 jit_solution(17696914821971063014)
XLA Ops:
  7.2 1.2 gather_fusion.1
  8.5 1.3 gather_fusion
  9.8 1.1 maximum_bitcast_fusion
  11.9 7.3 %all-to-all-start = ((bf16[2,8,32,2,128]{4,2,3,0,1:T(8,128)(2,1)}), bf16[2,8,32,2,128]{4,2,3,0,1:T(8,128)(2,1)S(1)}, u32[]{:S(2)}, u32[]{:S(2)}) async-start(bf16[2,8,32,2,128]{4,2,3,0,1:T(8,128)(2,1)} %bitcast_select_fusion), calls=%async_computation | async-start | bytes 524288 | tf_op jit(solution)/shard_map/all_to_all | solution.py:45
  20.1 7.9 %all-to-all-done = bf16[2,8,32,2,128]{4,2,3,0,1:T(8,128)(2,1)S(1)} async-done(((bf16[2,8,32,2,128]{4,2,3,0,1:T(8,128)(2,1)}), bf16[2,8,32,2,128]{4,2,3,0,1:T(8,128)(2,1)S(1)}, u32[]{:S(2)}, u32[]{:S(2)}) %all-to-all-start) | async-done | bytes 262176 | tf_op jit(solution)/shard_map/all_to_all | solution.py:45
  28.9 1.5 collective-permute-start
  30.4 10.4 %collective-permute-done = bf16[2,16,32,2,128]{4,2,3,0,1:T(8,128)(2,1)S(1)} collective-permute-done((bf16[2,16,32,2,128]{4,2,3,0,1:T(8,128)(2,1)S(1)}, bf16[2,16,32,2,128]{4,2,3,0,1:T(8,128)(2,1)S(1)}, u32[]{:S(2)}, u32[]{:S(2)}) %collective-permute-start) | collective-permute-done | bytes 524320 | tf_op jit(solution)/shard_map/ppermute | solution.py:14
  43.4 1.2 copy.18
  44.6 18.8 %collective-permute-done.1 = bf16[2,16,64,2,128]{4,2,3,0,1:T(8,128)(2,1)S(1)} collective-permute-done((bf16[2,16,64,2,128]{4,2,3,0,1:T(8,128)(2,1)S(1)}, bf16[2,16,64,2,128]{4,2,3,0,1:T(8,128)(2,1)S(1)}, u32[]{:S(2)}, u32[]{:S(2)}) %collective-permute-start.1) | collective-permute-done | bytes 1048608 | tf_op jit(solution)/shard_map/ppermute | solution.py:14
  73.5 1.1 fusion.154
  79.8 1.0 fusion.33
  91.1 1.1 scatter_fusion
  92.9 2.5 %fusion.35 = bf16[128,16,128]{2,0,1:T(8,128)(2,1)} fusion(bf16[128,16,128]{2,0,1:T(8,128)(2,1)} %fusion.33, f32[128,2048]{0,1:T(8,128)} %copy-done.23, f32[128]{0:T(128)S(1)} %fusion.67, f32[128]{0:T(128)S(1)} %get-tuple-element.18, bf16[2,2,2048,128]{3,2,1,0:T(8,128)(2,1)} %bitcast.347), kind=kOutput, calls=%fused_computation.72 | convolution fusion | flops 67911680 | bytes 1606656 | tf_op jit(solution)/shard_map/dot_general | solution.py:90
  96.6 1.0 fusion.39
  99.1 1.0 fusion.43
  101.5 1.0 fusion.47
  104.0 1.0 fusion.51
  105.2 1.0 fusion.53
  106.5 1.0 fusion.55
  108.6 1.0 fusion.59
  109.6 1.0 fusion.61
  110.6 1.0 fusion.63
  111.5 2.2 %copy.19 = bf16[128,16,128]{2,1,0:T(8,128)(2,1)} copy(bf16[128,16,128]{2,0,1:T(8,128)(2,1)} %fusion.63) | data formatting | bytes 1048576
  113.7 42.6 %reduce-scatter.2.cloned.1.call-done = f32[1,16,128]{2,1,0:T(8,128)} async-done(((f32[8,16,128]{2,1,0:T(8,128)}), f32[1,16,128]{2,1,0:T(8,128)}) %reduce-scatter.2.cloned.1.call-update) | async-done | bytes 8208 | tf_op jit(solution)/shard_map/reduce_scatter | solution.py:103
  (143 shorter events, 38.9 us)
Async XLA Ops:
  11.9 16.2 %all-to-all-start = ((bf16[2,8,32,2,128]{4,2,3,0,1:T(8,128)(2,1)}), bf16[2,8,32,2,128]{4,2,3,0,1:T(8,128)(2,1)S(1)}, u32[]{:S(2)}, u32[]{:S(2)}) async-start(bf16[2,8,32,2,128]{4,2,3,0,1:T(8,128)(2,1)} %bitcast_select_fusion), calls=%async_computation | async-start | bytes 524288 | tf_op jit(solution)/shard_map/all_to_all | solution.py:45
  19.1 137.2 %reduce-scatter.2.cloned.1.call-start = ((), (), s32[]{:S(2)}) async-start(), calls=%async_computation.2 | async-start | bytes 73728 | tf_op jit(solution)/shard_map/reduce_scatter | solution.py:103
  28.1 13.8 %copy-start = (s32[2]{0:T(128)S(1)}, s32[2]{0:T(128)}, u32[]{:S(2)}) copy-start(s32[2]{0:T(128)} %param.9) | copy-start | bytes 28
  28.1 14.4 %copy-start.26 = (s32[2,4]{1,0:T(2,128)S(1)}, s32[2,4]{1,0:T(2,128)}, u32[]{:S(2)}) copy-start(s32[2,4]{1,0:T(2,128)} %param.8) | copy-start | bytes 100
  28.9 11.9 %collective-permute-start = (bf16[2,16,32,2,128]{4,2,3,0,1:T(8,128)(2,1)S(1)}, bf16[2,16,32,2,128]{4,2,3,0,1:T(8,128)(2,1)S(1)}, u32[]{:S(2)}, u32[]{:S(2)}) collective-permute-start(bf16[2,16,32,2,128]{4,2,3,0,1:T(8,128)(2,1)S(1)} %select_bitcast_fusion), channel_id=1, source_target_pairs={{0,4},{4,0},{8,12},{12,8},{16,20},{20,16},{24,28},{28,24},{1,5},{5... | collective-permute-start | bytes 1572872 | tf_op jit(solution)/shard_map/ppermute | solution.py:14
  41.1 22.2 %collective-permute-start.1 = (bf16[2,16,64,2,128]{4,2,3,0,1:T(8,128)(2,1)S(1)}, bf16[2,16,64,2,128]{4,2,3,0,1:T(8,128)(2,1)S(1)}, u32[]{:S(2)}, u32[]{:S(2)}) collective-permute-start(bf16[2,16,64,2,128]{4,2,3,0,1:T(8,128)(2,1)S(1)} %maximum_select_fusion.1), channel_id=1, source_target_pairs={{0,8},{4,12},{8,0},{12,4},{16,24},{20,28},{24,16},{28,20},{1,9},{5... | collective-permute-start | bytes 3145736 | tf_op jit(solution)/shard_map/ppermute | solution.py:14
  64.4 15.4 %copy-start.24 = (bf16[2,16,128,2,128]{4,2,1,3,0:T(8,128)(2,1)}, bf16[2,16,128,2,128]{4,2,1,3,0:T(8,128)(2,1)S(1)}, u32[]{:S(2)}) copy-start(bf16[2,16,128,2,128]{4,2,1,3,0:T(8,128)(2,1)S(1)} %copy.17) | copy-start | bytes 6291460
  68.0 15.0 %copy-start.1 = (f32[128,2048]{0,1:T(8,128)}, f32[128,2048]{0,1:T(8,128)S(1)}, u32[]{:S(2)}) copy-start(f32[128,2048]{0,1:T(8,128)S(1)} %get-tuple-element.41) | copy-start | bytes 3145732
  68.9 14.8 %copy-start.3 = (f32[128,2048]{0,1:T(8,128)}, f32[128,2048]{0,1:T(8,128)S(1)}, u32[]{:S(2)}) copy-start(f32[128,2048]{0,1:T(8,128)S(1)} %get-tuple-element.39) | copy-start | bytes 3145732
  69.8 14.5 %copy-start.5 = (f32[128,2048]{0,1:T(8,128)}, f32[128,2048]{0,1:T(8,128)S(1)}, u32[]{:S(2)}) copy-start(f32[128,2048]{0,1:T(8,128)S(1)} %get-tuple-element.37) | copy-start | bytes 3145732
  70.8 14.3 %copy-start.7 = (f32[128,2048]{0,1:T(8,128)}, f32[128,2048]{0,1:T(8,128)S(1)}, u32[]{:S(2)}) copy-start(f32[128,2048]{0,1:T(8,128)S(1)} %get-tuple-element.35) | copy-start | bytes 3145732
  71.7 14.0 %copy-start.9 = (f32[128,2048]{0,1:T(8,128)}, f32[128,2048]{0,1:T(8,128)S(1)}, u32[]{:S(2)}) copy-start(f32[128,2048]{0,1:T(8,128)S(1)} %get-tuple-element.33) | copy-start | bytes 3145732
  72.6 13.8 %copy-start.11 = (f32[128,2048]{0,1:T(8,128)}, f32[128,2048]{0,1:T(8,128)S(1)}, u32[]{:S(2)}) copy-start(f32[128,2048]{0,1:T(8,128)S(1)} %get-tuple-element.31) | copy-start | bytes 3145732
  73.5 13.5 %copy-start.13 = (f32[128,2048]{0,1:T(8,128)}, f32[128,2048]{0,1:T(8,128)S(1)}, u32[]{:S(2)}) copy-start(f32[128,2048]{0,1:T(8,128)S(1)} %get-tuple-element.29) | copy-start | bytes 3145732
  74.6 13.3 %copy-start.15 = (f32[128,2048]{0,1:T(8,128)}, f32[128,2048]{0,1:T(8,128)S(1)}, u32[]{:S(2)}) copy-start(f32[128,2048]{0,1:T(8,128)S(1)} %get-tuple-element.27) | copy-start | bytes 3145732
  75.5 13.0 %copy-start.17 = (f32[128,2048]{0,1:T(8,128)}, f32[128,2048]{0,1:T(8,128)S(1)}, u32[]{:S(2)}) copy-start(f32[128,2048]{0,1:T(8,128)S(1)} %get-tuple-element.25) | copy-start | bytes 3145732
  76.4 12.8 %copy-start.19 = (f32[128,2048]{0,1:T(8,128)}, f32[128,2048]{0,1:T(8,128)S(1)}, u32[]{:S(2)}) copy-start(f32[128,2048]{0,1:T(8,128)S(1)} %get-tuple-element.23) | copy-start | bytes 3145732
  77.3 12.5 %copy-start.21 = (f32[128,2048]{0,1:T(8,128)}, f32[128,2048]{0,1:T(8,128)S(1)}, u32[]{:S(2)}) copy-start(f32[128,2048]{0,1:T(8,128)S(1)} %get-tuple-element.21) | copy-start | bytes 3145732
  78.2 12.3 %copy-start.23 = (f32[128,2048]{0,1:T(8,128)}, f32[128,2048]{0,1:T(8,128)S(1)}, u32[]{:S(2)}) copy-start(f32[128,2048]{0,1:T(8,128)S(1)} %get-tuple-element.19) | copy-start | bytes 3145732
  92.9 2.5 %copy-start.22 = (f32[128,2048]{0,1:T(8,128)S(1)}, f32[128,2048]{0,1:T(8,128)}, u32[]{:S(2)}) copy-start(f32[128,2048]{0,1:T(8,128)} %copy-done.21) | copy-start | bytes 3145732
  92.9 2.5 %copy-start.25 = (bf16[2,16,128,2,128]{4,2,1,3,0:T(8,128)(2,1)S(1)}, bf16[2,16,128,2,128]{4,2,1,3,0:T(8,128)(2,1)}, u32[]{:S(2)}) copy-start(bf16[2,16,128,2,128]{4,2,1,3,0:T(8,128)(2,1)} %copy-done.24) | copy-start | bytes 6291460
  95.4 1.2 copy-start.20
  101.5 1.2 copy-start.10
  106.5 1.2 copy-start.2
  (8 other events, 9.2 us)
Sparse Core Ops, SparseCore 0:
  93.0 63.2 reduce-scatter.1
where the time goes:
time: 164 us; the launch traced here: 163 us
  waiting for transfers between devices  79.7 us (49%)
  matrix products  31.6 us (19%)
  other arithmetic  16.6 us (10%)
  between operations  14.5 us (9%)
  local copies, waits for them, and re-layouts  11.3 us (7%)
  starting transfers between devices  9.52 us (6%)
    reduce_scatter x1, waiting for transfers between devices, on_device(): lax.psum_scatter(landing, 'ctx', scatter_dimension=0, tiled=True)  42.6 us
    ppermute x2, waiting for transfers between devices, from_partner(): return lax.ppermute(value, axis, pairs)  29.2 us
    dot_general x16, matrix products, on_device(): jnp.dot(attention.astype(jnp.bfloat16), value_head, preferred_element_typ...  16.9 us
    dot_general x16, matrix products, on_device(): lax.dot_general(grouped[:, kv_head, group_index], key_head, contract_last...  14.7 us
    all_to_all x1, waiting for transfers between devices, on_device(): lax.all_to_all(outgoing, 'ctx', split_axis=1, concat_axis=1, tiled=True)  7.9 us
    all_to_all x1, starting transfers between devices, on_device(): lax.all_to_all(outgoing, 'ctx', split_axis=1, concat_axis=1, tiled=True)  7.28 us
    unnamed x63, local copies, waits for them, and re-layouts  6.8 us
    reduce_sum x16, other arithmetic, on_device(): head_masses.append(jnp.sum(attention, axis=0).reshape(slot_total, BLOCK))  5.65 us
  transfers between devices with their start and end apart: 4, of which 4 were waited for; matrix products, arithmetic and copies ran while one was open for 13% of the time, Pallas kernels for 0%

commit v1 on v0

--- a/solution.py
+++ b/solution.py
@@ -1,11 +1,16 @@
+import functools
 import math
 
 import jax
 import jax.numpy as jnp
 from jax import lax
+from jax.experimental import pallas as pl
+from jax.experimental.pallas import tpu as pltpu
 from jax.sharding import PartitionSpec as P
 
 BLOCK = 512
+HIDDEN = -1e30
+SEGMENTS = 4
 
 
 def from_partner(value, axis, bit):
@@ -106,9 +111,285 @@
     return (attn_out, key_mass)
 
 
+def causal_kernel(
+    n, q_hbm, k_hbm, v_hbm, out_ref, mass_ref,
+    q_in, k_in, v_in, wide, q_all, k_all, v_all, scores, top, probs, mixed, mass, landed,
+    in_sem, k_line, k_pair, k_recv, v_line, v_pair, v_recv, m_send, m_recv,
+):
+    me = lax.axis_index("ctx")
+    level = me // 2
+    side = me % 2
+    levels = n // 2
+    tokens, heads, depth = q_in.shape
+    kv_total = heads // 8
+    rows = tokens * 8
+    partner = level * 2 + 1 - side
+    above = lax.rem(me + 2, n)
+    log2_scale = math.log2(math.e) / math.sqrt(depth)
+
+    copies_in = [
+        pltpu.make_async_copy(src, dst, in_sem.at[i])
+        for i, (src, dst) in enumerate(((k_hbm, k_in), (v_hbm, v_in), (q_hbm, q_in)))
+    ]
+    for copy in copies_in:
+        copy.start()
+    barrier = pltpu.get_barrier_semaphore()
+    for hop in range(1, n):
+        pl.semaphore_signal(
+            barrier, inc=1, device_id={"ctx": lax.rem(me + hop, n)},
+            device_id_type=pl.DeviceIdType.MESH,
+        )
+
+    def split_heads(source, target):
+        wide[...] = source[...].astype(jnp.float32)
+        for kv in range(kv_total):
+            target[me, kv] = wide[pl.ds(kv, tokens, stride=kv_total), :].astype(jnp.bfloat16)
+
+    def remote(ref, slot, send_sem, recv_sem, target):
+        return pltpu.make_async_remote_copy(
+            src_ref=ref.at[slot], dst_ref=ref.at[slot],
+            send_sem=send_sem.at[slot], recv_sem=recv_sem.at[slot],
+            device_id={"ctx": target}, device_id_type=pl.DeviceIdType.MESH,
+        )
+
+    def line_slot(back):
+        return (level - back) * 2 + side
+
+    def pair_slot(back):
+        return (level - back) * 2 + 1 - side
+
+    def has_line(back):
+        return level >= back
+
+    def has_pair(back):
+        return (level >= back) & (side == 1) if back == 0 else level >= back
+
+    def sends(ref, back, line_sem, pair_sem, recv_sem, act):
+        slot = line_slot(back)
+
+        @pl.when((level >= back) & (level < levels - 1))
+        def _():
+            act(remote(ref, slot, line_sem, recv_sem, above))
+
+        gives = (level >= back) & (side == 0) if back == 0 else level >= back
+
+        @pl.when(gives)
+        def _():
+            act(remote(ref, slot, pair_sem, recv_sem, partner))
+
+    def send_k(back, act):
+        sends(k_all, back, k_line, k_pair, k_recv, act)
+
+    def send_v(back, act):
+        sends(v_all, back, v_line, v_pair, v_recv, act)
+
+    def start(copy):
+        copy.start()
+
+    def arrive(ref, slot, send_sem, recv_sem):
+        remote(ref, slot, send_sem, recv_sem, partner).wait_recv()
+
+    def forward_k(back):
+        @pl.when(has_line(back))
+        def _():
+            arrive(k_all, line_slot(back), k_line, k_recv)
+
+        send_k(back, start)
+
+    def forward_v(back):
+        @pl.when(has_line(back))
+        def _():
+            arrive(v_all, line_slot(back), v_line, v_recv)
+
+        send_v(back, start)
+
+    def score(slot, own):
+        for kv in range(kv_total):
+            raw = lax.dot_general(
+                q_all[kv], k_all[slot, kv], (((1,), (1,)), ((), ())),
+                preferred_element_type=jnp.float32,
+            )
+            if own:
+                raw = raw.reshape(tokens, 8, tokens)
+                token = lax.broadcasted_iota(jnp.int32, raw.shape, 0)
+                key = lax.broadcasted_iota(jnp.int32, raw.shape, 2)
+                raw = jnp.where(key <= token, raw, HIDDEN).reshape(rows, tokens)
+                top[kv] = raw
+            else:
+                top[kv] = jnp.maximum(top[kv], raw)
+            scores[slot, kv] = raw
+
+    def score_line(back):
+        @pl.when(has_line(back))
+        def _():
+            score(line_slot(back), False)
+
+    def score_pair(back):
+        @pl.when(has_pair(back))
+        def _():
+            slot = pair_slot(back)
+            arrive(k_all, slot, k_pair, k_recv)
+            score(slot, False)
+
+    copies_in[0].wait()
+    split_heads(k_in, k_all)
+    pl.semaphore_wait(barrier, n - 1)
+    send_k(0, start)
+    copies_in[1].wait()
+    split_heads(v_in, v_all)
+    copies_in[2].wait()
+    for kv in range(kv_total):
+        q_part = q_in[...].astype(jnp.float32)[:, kv * 8 : kv * 8 + 8, :]
+        q_all[kv] = q_part.reshape(rows, depth).astype(jnp.bfloat16)
+    score(me, True)
+    for slot in range(1, n):
+
+        @pl.when(slot > me)
+        def _():
+            scores[slot] = jnp.full(scores.shape[1:], HIDDEN, jnp.float32)
+
+    for back in range(1, levels):
+        forward_k(back)
+        if back == 1:
+            send_v(0, start)
+        score_line(back)
+        score_pair(back - 1)
+    score_pair(levels - 1)
+
+    mass[...] = jnp.zeros_like(mass)
+    part_rows = 128
+    parts = rows // part_rows
+    total = kv_total * parts
+
+    def soften(index, carry):
+        kv = index // parts
+        at = pl.ds(pl.multiple_of((index % parts) * part_rows, part_rows), part_rows)
+        highest = jnp.max(top[kv, at, :], axis=-1, keepdims=True) * log2_scale
+        summed = jnp.zeros((part_rows, tokens), jnp.float32)
+        for slot in range(n):
+            raised = jnp.exp2(scores[slot, kv, at, :] * log2_scale - highest)
+            scores[slot, kv, at, :] = raised
+            summed = summed + raised
+        inverse = 1.0 / jnp.sum(summed, axis=-1, keepdims=True)
+        for slot in range(n):
+            attention = scores[slot, kv, at, :] * inverse
+            probs[slot, kv, at, :] = attention.astype(jnp.bfloat16)
+            mass[slot, kv] += jnp.sum(attention.reshape(part_rows // 8, 8, tokens), axis=0)
+        return carry
+
+    for segment in range(SEGMENTS):
+        if 1 + segment < levels:
+            forward_v(1 + segment)
+        lax.fori_loop(segment * total // SEGMENTS, (segment + 1) * total // SEGMENTS, soften, 0)
+
+    def mass_copy(source, target):
+        return pltpu.make_async_remote_copy(
+            src_ref=mass.at[target], dst_ref=landed.at[source],
+            send_sem=m_send.at[target], recv_sem=m_recv.at[source],
+            device_id={"ctx": target}, device_id_type=pl.DeviceIdType.MESH,
+        )
+
+    for slot in range(n - 1):
+
+        @pl.when(slot < me)
+        def _():
+            mass_copy(me, slot).start()
+
+    def mix(slot, first):
+        for kv in range(kv_total):
+            piece = jnp.dot(probs[slot, kv], v_all[slot, kv], preferred_element_type=jnp.float32)
+            mixed[kv] = piece if first else mixed[kv] + piece
+
+    def mix_line(back):
+        @pl.when(has_line(back))
+        def _():
+            mix(line_slot(back), False)
+
+    def mix_pair(back):
+        @pl.when(has_pair(back))
+        def _():
+            slot = pair_slot(back)
+            arrive(v_all, slot, v_pair, v_recv)
+            mix(slot, False)
+
+    mix(me, True)
+    for back in range(1, levels):
+        mix_line(back)
+        mix_pair(back - 1)
+    mix_pair(levels - 1)
+    out_ref[...] = jnp.concatenate(
+        [mixed[kv].reshape(tokens, 8, depth) for kv in range(kv_total)], axis=1
+    ).astype(out_ref.dtype)
+
+    mass_ref[...] = jnp.concatenate([mass[me, kv] for kv in range(kv_total)], axis=0)
+    for slot in range(1, n):
+
+        @pl.when(slot > me)
+        def _():
+            mass_copy(slot, me * 0 + partner).wait_recv()
+            mass_ref[...] += jnp.concatenate([landed[slot, kv] for kv in range(kv_total)], axis=0)
+
+    def wait_send(copy):
+        copy.wait_send()
+
+    for back in range(levels):
+        send_k(back, wait_send)
+        send_v(back, wait_send)
+    for slot in range(n - 1):
+
+        @pl.when(slot < me)
+        def _():
+            mass_copy(me, slot).wait_send()
+
+
+def causal_step(n, queries, key_states, value_states):
+    tokens, heads, depth = queries.shape
+    kv_total = key_states.shape[1]
+    rows = tokens * 8
+    f32, bf16 = jnp.float32, jnp.bfloat16
+    dma = pltpu.SemaphoreType.DMA
+    return pl.pallas_call(
+        functools.partial(causal_kernel, n),
+        out_shape=(
+            jax.ShapeDtypeStruct((tokens, heads, depth), bf16),
+            jax.ShapeDtypeStruct((heads, tokens), f32),
+        ),
+        in_specs=[pl.BlockSpec(memory_space=pl.ANY)] * 3,
+        out_specs=[pl.BlockSpec(memory_space=pltpu.VMEM)] * 2,
+        scratch_shapes=[
+            pltpu.VMEM((tokens, heads, depth), bf16),
+            pltpu.VMEM((tokens * kv_total, depth), bf16),
+            pltpu.VMEM((tokens * kv_total, depth), bf16),
+            pltpu.VMEM((tokens * kv_total, depth), f32),
+            pltpu.VMEM((kv_total, rows, depth), bf16),
+            pltpu.VMEM((n, kv_total, tokens, depth), bf16),
+            pltpu.VMEM((n, kv_total, tokens, depth), bf16),
+            pltpu.VMEM((n, kv_total, rows, tokens), f32),
+            pltpu.VMEM((kv_total, rows, tokens), f32),
+            pltpu.VMEM((n, kv_total, rows, tokens), bf16),
+            pltpu.VMEM((kv_total, rows, depth), f32),
+            pltpu.VMEM((n, kv_total, 8, tokens), f32),
+            pltpu.VMEM((n, kv_total, 8, tokens), f32),
+            dma((3,)), dma((n,)), dma((n,)), dma((n,)), dma((n,)), dma((n,)), dma((n,)),
+            dma((n,)), dma((n,)),
+        ],
+        compiler_params=pltpu.CompilerParams(
+            collective_id=0, has_side_effects=True, vmem_limit_bytes=40 * 1024 * 1024
+        ),
+    )(
+        queries,
+        key_states.reshape(tokens * kv_total, depth),
+        value_states.reshape(tokens * kv_total, depth),
+    )
+
+
 def solution(mesh):
     in_specs = (P("ctx", "head", None), P("ctx", "head", None), P("ctx", "head", None), P(), P())
     out_specs = (P("ctx", "head", None), P("head", "ctx"))
-    return jax.shard_map(
-        on_device, mesh=mesh, in_specs=in_specs, out_specs=out_specs, check_vma=False
-    )
+
+    def step(queries, key_states, value_states, chosen, valid_count):
+        if chosen.shape[0] <= 2 and mesh.shape["ctx"] % 2 == 0:
+            return causal_step(mesh.shape["ctx"], queries, key_states, value_states)
+        return on_device(queries, key_states, value_states, chosen, valid_count)
+
+    return jax.shard_map(step, mesh=mesh, in_specs=in_specs, out_specs=out_specs, check_vma=False)

time: 164 us -> 35.1 us (0.21)
  waiting for transfers between devices: 79.7 us -> 0 us
  matrix products: 31.6 us -> 0 us
  Pallas kernels: 0 us -> 30.1 us
  other arithmetic: 16.6 us -> 0 us
  between operations: 14.5 us -> 0.65 us
  starting transfers between devices: 9.52 us -> 0 us
  local copies, waits for them, and re-layouts: 11.3 us -> 4.11 us
    reduce_scatter x1 -> x0, waiting for transfers between devices: 42.6 us -> none  [on_device(): lax.psum_scatter(landing, 'ctx', scatter_dimension=0, tiled=True)]
    dot_general x32 -> x0, matrix products: 31.6 us -> none  [the longest x16 16.9 us: on_device(): jnp.dot(attention.astype(jnp.bfloat16), value_head, preferred_element_typ...]
    pallas_call x0 -> x1, Pallas kernels: none -> 30.1 us  [causal_step(): pl.pallas_call(functools.partial(causal_kernel, n), out_shape=(jax.ShapeD...]
    ppermute x2 -> x0, waiting for transfers between devices: 29.2 us -> none  [from_partner(): return lax.ppermute(value, axis, pairs)]
    reduce_sum x32 -> x0, other arithmetic: 10.6 us -> none  [the longest x16 5.65 us: on_device(): head_masses.append(jnp.sum(attention, axis=0).reshape(slot_total, BLOCK))]
    all_to_all x1 -> x0, waiting for transfers between devices: 7.9 us -> none  [on_device(): lax.all_to_all(outgoing, 'ctx', split_axis=1, concat_axis=1, tiled=True)]
    all_to_all x1 -> x0, starting transfers between devices: 7.28 us -> none  [on_device(): lax.all_to_all(outgoing, 'ctx', split_axis=1, concat_axis=1, tiled=True)]
    gather x3 -> x0, local copies, waits for them, and re-layouts: 3.19 us -> none  [the longest x1 1.3 us: on_device(): valid_count[owners][:, None]]
  transfers between devices with their start and end apart: 4 -> 0, of which waited for: 4 -> 0; matrix products, arithmetic and copies ran while one was open for 13% -> 0% of each run, Pallas kernels for 0% -> 0%
where the time goes in v1:
time: 35.1 us; the launch traced here: 34.8 us
  Pallas kernels  30.1 us (86%)
  local copies, waits for them, and re-layouts  4.11 us (12%)
  between operations  0.65 us (2%)
    pallas_call x1, Pallas kernels, causal_step(): pl.pallas_call(functools.partial(causal_kernel, n), out_shape=(jax.ShapeD...  30.1 us
    unnamed x8, local copies, waits for them, and re-layouts  4.11 us

profile of v1, /device:TPU:0, one launch (start us, length us, event | category | flops | bytes accessed | tf_op | source)
XLA Modules:
  0.0 34.8 jit_solution(14447018277340563776)
XLA Ops:
  0.6 0.0 copy-start
  0.6 1.0 %copy-done = bf16[128,16,128]{2,1,0:T(8,128)(2,1)S(1)} copy-done((bf16[128,16,128]{2,1,0:T(8,128)(2,1)S(1)}, bf16[128,16,128]{2,1,0:T(8,128)(2,1)}, u32[]{:S(2)}) %copy-start) | copy-done | bytes 524312
  1.7 0.0 copy-start.1
  1.7 0.8 %copy-done.1 = bf16[128,2,128]{2,1,0:T(2,128)(2,1)S(1)} copy-done((bf16[128,2,128]{2,1,0:T(2,128)(2,1)S(1)}, bf16[128,2,128]{2,1,0:T(2,128)(2,1)}, u32[]{:S(2)}) %copy-start.1) | copy-done | bytes 65560
  2.5 0.0 copy-start.2
  2.5 0.8 %copy-done.2 = bf16[128,2,128]{2,1,0:T(2,128)(2,1)S(1)} copy-done((bf16[128,2,128]{2,1,0:T(2,128)(2,1)S(1)}, bf16[128,2,128]{2,1,0:T(2,128)(2,1)}, u32[]{:S(2)}) %copy-start.2) | copy-done | bytes 65560
  3.4 30.1 %shard_map.50 = (bf16[128,16,128]{2,1,0:T(8,128)(2,1)S(1)}, f32[16,128]{1,0:T(8,128)S(1)}) custom-call(bf16[128,16,128]{2,1,0:T(8,128)(2,1)S(1)} %copy-done, bf16[256,128]{1,0:T(8,128)(2,1)S(1)} %bitcast.2, bf16[256,128]{1,0:T(8,128)(2,1)S(1)} %bitcast.3), custom_call_target="tpu_custom_call" | custom-call | tf_op jit(solution)/shard_map/pallas_call | solution.py:351
  33.4 0.8 %copy.7 = bf16[128,16,128]{2,1,0:T(8,128)(2,1)} copy(bf16[128,16,128]{2,1,0:T(8,128)(2,1)S(1)} %get-tuple-element.4) | data formatting | bytes 1048576
  34.2 0.6 %copy.8 = f32[16,128]{1,0:T(8,128)} copy(f32[16,128]{1,0:T(8,128)S(1)} %get-tuple-element.5) | data formatting | bytes 16384
Async XLA Ops:
  0.6 1.0 %copy-start = (bf16[128,16,128]{2,1,0:T(8,128)(2,1)S(1)}, bf16[128,16,128]{2,1,0:T(8,128)(2,1)}, u32[]{:S(2)}) copy-start(bf16[128,16,128]{2,1,0:T(8,128)(2,1)} %q_hbm.1) | copy-start | bytes 1572868
  1.7 0.8 %copy-start.1 = (bf16[128,2,128]{2,1,0:T(2,128)(2,1)S(1)}, bf16[128,2,128]{2,1,0:T(2,128)(2,1)}, u32[]{:S(2)}) copy-start(bf16[128,2,128]{2,1,0:T(2,128)(2,1)} %param.6) | copy-start | bytes 196612
  2.5 0.8 %copy-start.2 = (bf16[128,2,128]{2,1,0:T(2,128)(2,1)S(1)}, bf16[128,2,128]{2,1,0:T(2,128)(2,1)}, u32[]{:S(2)}) copy-start(bf16[128,2,128]{2,1,0:T(2,128)(2,1)} %param.7) | copy-start | bytes 196612

commit v2 on v1

--- a/solution.py
+++ b/solution.py
@@ -124,7 +124,6 @@
     kv_total = heads // 8
     rows = tokens * 8
     partner = level * 2 + 1 - side
-    above = lax.rem(me + 2, n)
     log2_scale = math.log2(math.e) / math.sqrt(depth)
 
     copies_in = [
@@ -145,10 +144,10 @@
         for kv in range(kv_total):
             target[me, kv] = wide[pl.ds(kv, tokens, stride=kv_total), :].astype(jnp.bfloat16)
 
-    def remote(ref, slot, send_sem, recv_sem, target):
+    def remote(ref, slot, send_sem, recv_sem, target, offset=0):
         return pltpu.make_async_remote_copy(
             src_ref=ref.at[slot], dst_ref=ref.at[slot],
-            send_sem=send_sem.at[slot], recv_sem=recv_sem.at[slot],
+            send_sem=send_sem.at[offset + slot], recv_sem=recv_sem.at[slot],
             device_id={"ctx": target}, device_id_type=pl.DeviceIdType.MESH,
         )
 
@@ -167,9 +166,12 @@
     def sends(ref, back, line_sem, pair_sem, recv_sem, act):
         slot = line_slot(back)
 
-        @pl.when((level >= back) & (level < levels - 1))
-        def _():
-            act(remote(ref, slot, line_sem, recv_sem, above))
+        for hop in (1, 2) if back % 2 == 0 else ():
+
+            @pl.when((level >= back) & (level + hop < levels))
+            def _():
+                target = lax.rem(me + 2 * hop, n)
+                act(remote(ref, slot, line_sem, recv_sem, target, (hop - 1) * n))
 
         gives = (level >= back) & (side == 0) if back == 0 else level >= back
 
@@ -354,7 +356,7 @@
             jax.ShapeDtypeStruct((tokens, heads, depth), bf16),
             jax.ShapeDtypeStruct((heads, tokens), f32),
         ),
-        in_specs=[pl.BlockSpec(memory_space=pl.ANY)] * 3,
+        in_specs=[pl.BlockSpec(memory_space=pltpu.HBM)] * 3,
         out_specs=[pl.BlockSpec(memory_space=pltpu.VMEM)] * 2,
         scratch_shapes=[
             pltpu.VMEM((tokens, heads, depth), bf16),
@@ -370,11 +372,11 @@
             pltpu.VMEM((kv_total, rows, depth), f32),
             pltpu.VMEM((n, kv_total, 8, tokens), f32),
             pltpu.VMEM((n, kv_total, 8, tokens), f32),
-            dma((3,)), dma((n,)), dma((n,)), dma((n,)), dma((n,)), dma((n,)), dma((n,)),
+            dma((3,)), dma((2 * n,)), dma((n,)), dma((n,)), dma((2 * n,)), dma((n,)), dma((n,)),
             dma((n,)), dma((n,)),
         ],
         compiler_params=pltpu.CompilerParams(
-            collective_id=0, has_side_effects=True, vmem_limit_bytes=40 * 1024 * 1024
+            collective_id=0, has_side_effects=True, vmem_limit_bytes=62 * 1024 * 1024
         ),
     )(
         queries,

time: 35.1 us -> 33.1 us (0.943)
  local copies, waits for them, and re-layouts: 4.11 us -> 2.48 us
    unnamed x8 -> x4, local copies, waits for them, and re-layouts: 4.11 us -> 2.48 us
where the time goes in v2:
time: 33.1 us; the launch traced here: 33 us
  Pallas kernels  29.9 us (90%)
  local copies, waits for them, and re-layouts  2.48 us (7%)
  between operations  0.65 us (2%)
    pallas_call x1, Pallas kernels, causal_step(): pl.pallas_call(functools.partial(causal_kernel, n), out_shape=(jax.ShapeD...  29.9 us
    unnamed x4, local copies, waits for them, and re-layouts  2.48 us

profile of v2, /device:TPU:0, one launch (start us, length us, event | category | flops | bytes accessed | tf_op | source)
XLA Modules:
  0.0 33.0 jit_solution(7261148635017864802)
XLA Ops:
  0.6 29.9 %shard_map.50 = (bf16[128,16,128]{2,1,0:T(8,128)(2,1)}, f32[16,128]{1,0:T(8,128)}) custom-call(bf16[128,16,128]{2,1,0:T(8,128)(2,1)} %q_hbm.1, bf16[256,128]{1,0:T(8,128)(2,1)} %bitcast.2, bf16[256,128]{1,0:T(8,128)(2,1)} %bitcast.3), custom_call_target="tpu_custom_call" | custom-call | tf_op jit(solution)/shard_map/pallas_call | solution.py:353
  30.5 0.0 copy-start
  30.5 1.9 %copy.7 = bf16[128,16,128]{2,1,0:T(8,128)(2,1)} copy(bf16[128,16,128]{2,1,0:T(8,128)(2,1)} %get-tuple-element.4) | data formatting | bytes 1048576
  32.4 0.0 copy-done
  32.4 0.6 %copy.8 = f32[16,128]{1,0:T(8,128)} copy(f32[16,128]{1,0:T(8,128)S(1)} %copy-done) | data formatting | bytes 16384
Async XLA Ops:
  30.5 1.9 %copy-start = (f32[16,128]{1,0:T(8,128)S(1)}, f32[16,128]{1,0:T(8,128)}, u32[]{:S(2)}) copy-start(f32[16,128]{1,0:T(8,128)} %get-tuple-element.5) | copy-start | bytes 24580

commit v3 on v2

--- a/solution.py
+++ b/solution.py
@@ -144,10 +144,10 @@
         for kv in range(kv_total):
             target[me, kv] = wide[pl.ds(kv, tokens, stride=kv_total), :].astype(jnp.bfloat16)
 
-    def remote(ref, slot, send_sem, recv_sem, target, offset=0):
+    def remote(ref, slot, kv, send_sem, recv_sem, target, hop=0):
         return pltpu.make_async_remote_copy(
-            src_ref=ref.at[slot], dst_ref=ref.at[slot],
-            send_sem=send_sem.at[offset + slot], recv_sem=recv_sem.at[slot],
+            src_ref=ref.at[slot, kv], dst_ref=ref.at[slot, kv],
+            send_sem=send_sem.at[hop, slot, kv], recv_sem=recv_sem.at[slot, kv],
             device_id={"ctx": target}, device_id_type=pl.DeviceIdType.MESH,
         )
 
@@ -163,7 +163,7 @@
     def has_pair(back):
         return (level >= back) & (side == 1) if back == 0 else level >= back
 
-    def sends(ref, back, line_sem, pair_sem, recv_sem, act):
+    def sends(ref, back, kv, line_sem, pair_sem, recv_sem, act):
         slot = line_slot(back)
 
         for hop in (1, 2) if back % 2 == 0 else ():
@@ -171,39 +171,49 @@
             @pl.when((level >= back) & (level + hop < levels))
             def _():
                 target = lax.rem(me + 2 * hop, n)
-                act(remote(ref, slot, line_sem, recv_sem, target, (hop - 1) * n))
+                act(remote(ref, slot, kv, line_sem, recv_sem, target, hop - 1))
 
         gives = (level >= back) & (side == 0) if back == 0 else level >= back
 
         @pl.when(gives)
         def _():
-            act(remote(ref, slot, pair_sem, recv_sem, partner))
+            act(remote(ref, slot, kv, pair_sem, recv_sem, partner))
 
     def send_k(back, act):
-        sends(k_all, back, k_line, k_pair, k_recv, act)
+        for kv in range(kv_total):
+            sends(k_all, back, kv, k_line, k_pair, k_recv, act)
 
     def send_v(back, act):
-        sends(v_all, back, v_line, v_pair, v_recv, act)
+        for kv in range(kv_total):
+            sends(v_all, back, kv, v_line, v_pair, v_recv, act)
 
     def start(copy):
         copy.start()
 
+    def arrive_part(ref, slot, kv, send_sem, recv_sem):
+        remote(ref, slot, kv, send_sem, recv_sem, partner).wait_recv()
+
     def arrive(ref, slot, send_sem, recv_sem):
-        remote(ref, slot, send_sem, recv_sem, partner).wait_recv()
+        for kv in range(kv_total):
+            arrive_part(ref, slot, kv, send_sem, recv_sem)
 
     def forward_k(back):
-        @pl.when(has_line(back))
-        def _():
-            arrive(k_all, line_slot(back), k_line, k_recv)
-
-        send_k(back, start)
+        for kv in range(kv_total):
+
+            @pl.when(has_line(back))
+            def _():
+                arrive_part(k_all, line_slot(back), kv, k_line, k_recv)
+
+            sends(k_all, back, kv, k_line, k_pair, k_recv, start)
 
     def forward_v(back):
-        @pl.when(has_line(back))
-        def _():
-            arrive(v_all, line_slot(back), v_line, v_recv)
-
-        send_v(back, start)
+        for kv in range(kv_total):
+
+            @pl.when(has_line(back))
+            def _():
+                arrive_part(v_all, line_slot(back), kv, v_line, v_recv)
+
+            sends(v_all, back, kv, v_line, v_pair, v_recv, start)
 
     def score(slot, own):
         for kv in range(kv_total):
@@ -211,6 +221,7 @@
                 q_all[kv], k_all[slot, kv], (((1,), (1,)), ((), ())),
                 preferred_element_type=jnp.float32,
             )
+            raw = raw * log2_scale
             if own:
                 raw = raw.reshape(tokens, 8, tokens)
                 token = lax.broadcasted_iota(jnp.int32, raw.shape, 0)
@@ -255,21 +266,25 @@
         if back == 1:
             send_v(0, start)
         score_line(back)
-        score_pair(back - 1)
+        if back >= 2:
+            score_pair(back - 2)
+    if levels > 1:
+        forward_v(1)
+        score_pair(levels - 2)
     score_pair(levels - 1)
 
     mass[...] = jnp.zeros_like(mass)
-    part_rows = 128
+    part_rows = 512
     parts = rows // part_rows
     total = kv_total * parts
 
     def soften(index, carry):
         kv = index // parts
         at = pl.ds(pl.multiple_of((index % parts) * part_rows, part_rows), part_rows)
-        highest = jnp.max(top[kv, at, :], axis=-1, keepdims=True) * log2_scale
+        highest = jnp.max(top[kv, at, :], axis=-1, keepdims=True)
         summed = jnp.zeros((part_rows, tokens), jnp.float32)
         for slot in range(n):
-            raised = jnp.exp2(scores[slot, kv, at, :] * log2_scale - highest)
+            raised = jnp.exp2(scores[slot, kv, at, :] - highest)
             scores[slot, kv, at, :] = raised
             summed = summed + raised
         inverse = 1.0 / jnp.sum(summed, axis=-1, keepdims=True)
@@ -280,8 +295,8 @@
         return carry
 
     for segment in range(SEGMENTS):
-        if 1 + segment < levels:
-            forward_v(1 + segment)
+        if 2 + segment < levels:
+            forward_v(2 + segment)
         lax.fori_loop(segment * total // SEGMENTS, (segment + 1) * total // SEGMENTS, soften, 0)
 
     def mass_copy(source, target):
@@ -372,7 +387,8 @@
             pltpu.VMEM((kv_total, rows, depth), f32),
             pltpu.VMEM((n, kv_total, 8, tokens), f32),
             pltpu.VMEM((n, kv_total, 8, tokens), f32),
-            dma((3,)), dma((2 * n,)), dma((n,)), dma((n,)), dma((2 * n,)), dma((n,)), dma((n,)),
+            dma((3,)), dma((2, n, kv_total)), dma((1, n, kv_total)), dma((n, kv_total)),
+            dma((2, n, kv_total)), dma((1, n, kv_total)), dma((n, kv_total)),
             dma((n,)), dma((n,)),
         ],
         compiler_params=pltpu.CompilerParams(

time: 33.1 us -> 31.2 us (0.943)
  Pallas kernels: 29.9 us -> 27.9 us
    pallas_call x1, Pallas kernels: 29.9 us -> 27.9 us  [causal_step(): pl.pallas_call(functools.partial(causal_kernel, n), out_shape=(jax.ShapeD...]
where the time goes in v3:
time: 31.2 us; the launch traced here: 31 us
  Pallas kernels  27.9 us (89%)
  local copies, waits for them, and re-layouts  2.48 us (8%)
  between operations  0.65 us (2%)
    pallas_call x1, Pallas kernels, causal_step(): pl.pallas_call(functools.partial(causal_kernel, n), out_shape=(jax.ShapeD...  27.9 us
    unnamed x4, local copies, waits for them, and re-layouts  2.48 us

profile of v3, /device:TPU:0, one launch (start us, length us, event | category | flops | bytes accessed | tf_op | source)
XLA Modules:
  0.0 31.0 jit_solution(76861797213221003)
XLA Ops:
  0.6 27.9 %shard_map.50 = (bf16[128,16,128]{2,1,0:T(8,128)(2,1)}, f32[16,128]{1,0:T(8,128)}) custom-call(bf16[128,16,128]{2,1,0:T(8,128)(2,1)} %q_hbm.1, bf16[256,128]{1,0:T(8,128)(2,1)} %bitcast.2, bf16[256,128]{1,0:T(8,128)(2,1)} %bitcast.3), custom_call_target="tpu_custom_call" | custom-call | tf_op jit(solution)/shard_map/pallas_call | solution.py:368
  28.5 0.0 copy-start
  28.5 1.9 %copy.7 = bf16[128,16,128]{2,1,0:T(8,128)(2,1)} copy(bf16[128,16,128]{2,1,0:T(8,128)(2,1)} %get-tuple-element.4) | data formatting | bytes 1048576
  30.4 0.0 copy-done
  30.4 0.6 %copy.8 = f32[16,128]{1,0:T(8,128)} copy(f32[16,128]{1,0:T(8,128)S(1)} %copy-done) | data formatting | bytes 16384
Async XLA Ops:
  28.5 1.9 %copy-start = (f32[16,128]{1,0:T(8,128)S(1)}, f32[16,128]{1,0:T(8,128)}, u32[]{:S(2)}) copy-start(f32[16,128]{1,0:T(8,128)} %get-tuple-element.5) | copy-start | bytes 24580

commit v4 on v3

--- a/solution.py
+++ b/solution.py
@@ -10,7 +10,7 @@
 
 BLOCK = 512
 HIDDEN = -1e30
-SEGMENTS = 4
+SEGMENTS = 2
 
 
 def from_partner(value, axis, bit):
@@ -274,7 +274,7 @@
     score_pair(levels - 1)
 
     mass[...] = jnp.zeros_like(mass)
-    part_rows = 512
+    part_rows = 1024
     parts = rows // part_rows
     total = kv_total * parts
 
@@ -295,8 +295,8 @@
         return carry
 
     for segment in range(SEGMENTS):
-        if 2 + segment < levels:
-            forward_v(2 + segment)
+        for back in range(2 + segment, levels, SEGMENTS):
+            forward_v(back)
         lax.fori_loop(segment * total // SEGMENTS, (segment + 1) * total // SEGMENTS, soften, 0)
 
     def mass_copy(source, target):

time: 31.2 us -> 31 us (level)
  no operation moved by 1% of the time
where the time goes in v4:
time: 31 us; the launch traced here: 30.9 us
  Pallas kernels  27.8 us (90%)
  local copies, waits for them, and re-layouts  2.48 us (8%)
  between operations  0.65 us (2%)
    pallas_call x1, Pallas kernels, causal_step(): pl.pallas_call(functools.partial(causal_kernel, n), out_shape=(jax.ShapeD...  27.8 us
    unnamed x4, local copies, waits for them, and re-layouts  2.48 us

profile of v4, /device:TPU:0, one launch (start us, length us, event | category | flops | bytes accessed | tf_op | source)
XLA Modules:
  0.0 30.9 jit_solution(11353445954014340905)
XLA Ops:
  0.6 27.8 %shard_map.50 = (bf16[128,16,128]{2,1,0:T(8,128)(2,1)}, f32[16,128]{1,0:T(8,128)}) custom-call(bf16[128,16,128]{2,1,0:T(8,128)(2,1)} %q_hbm.1, bf16[256,128]{1,0:T(8,128)(2,1)} %bitcast.2, bf16[256,128]{1,0:T(8,128)(2,1)} %bitcast.3), custom_call_target="tpu_custom_call" | custom-call | tf_op jit(solution)/shard_map/pallas_call | solution.py:368
  28.4 0.0 copy-start
  28.4 1.9 %copy.7 = bf16[128,16,128]{2,1,0:T(8,128)(2,1)} copy(bf16[128,16,128]{2,1,0:T(8,128)(2,1)} %get-tuple-element.4) | data formatting | bytes 1048576
  30.3 0.0 copy-done
  30.3 0.6 %copy.8 = f32[16,128]{1,0:T(8,128)} copy(f32[16,128]{1,0:T(8,128)S(1)} %copy-done) | data formatting | bytes 16384
Async XLA Ops:
  28.4 1.9 %copy-start = (f32[16,128]{1,0:T(8,128)S(1)}, f32[16,128]{1,0:T(8,128)}, u32[]{:S(2)}) copy-start(f32[16,128]{1,0:T(8,128)} %get-tuple-element.5) | copy-start | bytes 24580
